TPU v7x, 128 devices: a whole 4x4x4 slice. The times are simulated.
128 devices in a mesh: row: 8 (over z, core), col: 16 (over y, x).
Axes of the slice: x: 4, y: 4, z: 4, core: 2. Of those that a mesh axis runs over, the one named last changes fastest.
Arguments:
- singles: bfloat16 [1024, 384], P('row', 'col'), may hold values from -6 to 6
- pair_in: bfloat16 [1024, 1024, 128], P('row', 'col'), may hold values from -6 to 6
- proj_weight: bfloat16 [384, 256], P('col'), may hold values from -0.3125 to 0.3125
- gain_first: float32 [128], replicated, may hold values from 0.1 to 1.9
- first_in: bfloat16 [128, 1024], replicated, may hold values from -0.5 to 0.5
- first_out: bfloat16 [512, 128], replicated, may hold values from -0.25 to 0.25
- gain_second: float32 [128], replicated, may hold values from 0.1 to 1.9
- second_in: bfloat16 [128, 1024], replicated, may hold values from -0.5 to 0.5
- second_out: bfloat16 [512, 128], replicated, may hold values from -0.25 to 0.25
- head_weight: bfloat16 [128, 64], replicated, may hold values from -1.5 to 1.5
- pae_bins: int32 [1024, 1024], P('row', 'col'), may hold values from 0 to 63
- chain_perm: int32 [1024], replicated, may hold values from 0 to 1023, as said below
- resolved_counts: int32 [8, 16], P('row'), may hold values from 1 to 256, 2048 in all within a row
- tile_order: int32 [8, 4096], P('row', 'col'), may hold values from 0 to 255, as said below
Outputs:
- pair_grad: bfloat16 [1024, 1024, 128], P('row', 'col')
- single_grad: float32 [1024, 384], P('row', 'col')
- second_in_grad: float32 [128, 1024], replicated
- second_out_grad: float32 [512, 128], replicated
- head_grad: float32 [128, 64], replicated
Inputs may be any that keep to these rules, and one draw needn't show every extreme that they name: chain_perm maps every aligned group of 64 tokens onto itself, moving whole aligned runs of 16 tokens and keeping the order inside a run. Each row of resolved_counts sums to 2048, and its largest entry is 256. In each row of tile_order, entries b * 256 to (b + 1) * 256 - 1 are a permutation of 0 to 255.
All inputs are finite; a program needn't handle non-finite values.
Results may differ from a plain program's by a relative error of at most 0.011.
Values may be sent and summed in bfloat16 or wider, within the bound.
A program may use at most 64 MiB of HBM per device.

v0:
```python
import jax
import jax.numpy as jnp
from jax import lax
from jax.sharding import PartitionSpec as P

TILE = 32


def contract(left_op, right_op, left_dim, right_dim):
    return lax.dot_general(
        left_op,
        right_op,
        (((left_dim,), (right_dim,)), ((), ())),
        preferred_element_type=jnp.float32,
    )


def block_size(extent, per_item, limit):
    best = 1
    for candidate in range(1, extent + 1):
        if extent % candidate == 0 and candidate * per_item <= limit:
            best = candidate
    return best


def transition_forward(start_z, gain_vec, w_in, w_out):
    hidden_units = w_out.shape[0]
    average = jnp.mean(start_z, axis=-1, keepdims=True)
    centred = start_z - average
    scaling = lax.rsqrt(jnp.mean(centred * centred, axis=-1, keepdims=True) + 1e-05)
    normed = centred * scaling
    inputs = (normed * gain_vec).astype(jnp.bfloat16)
    gate_up = jnp.dot(inputs, w_in, preferred_element_type=jnp.float32)
    gate_part = gate_up[:, :hidden_units]
    up_part = gate_up[:, hidden_units:]
    gate_sig = jax.nn.sigmoid(gate_part)
    hidden_act = (gate_part * gate_sig * up_part).astype(jnp.bfloat16)
    result = jnp.dot(hidden_act, w_out, preferred_element_type=jnp.float32)
    return (result, (normed, scaling, inputs, gate_part, up_part, gate_sig, hidden_act))


def transition_backward(saved, grad_out, gain_vec, w_in, w_out, with_weights):
    normed, scaling, inputs, gate_part, up_part, gate_sig, hidden_act = saved
    grad_hidden = contract(grad_out, w_out, 1, 1)
    grad_gate = grad_hidden * up_part * gate_sig * (1.0 + gate_part * (1.0 - gate_sig))
    grad_up = grad_hidden * gate_part * gate_sig
    grad_both = jnp.concatenate([grad_gate, grad_up], axis=1).astype(jnp.bfloat16)
    grad_normed = contract(grad_both, w_in, 1, 1) * gain_vec
    grad_field = scaling * (
        grad_normed
        - jnp.mean(grad_normed, axis=-1, keepdims=True)
        - normed * jnp.mean(grad_normed * normed, axis=-1, keepdims=True)
    )
    if with_weights:
        return (grad_field, contract(inputs, grad_both, 0, 0), contract(hidden_act, grad_out, 0, 0))
    return (grad_field, None, None)


def head_step(rounded_z, targets, keep_mask, head_weight):
    logits = jnp.dot(rounded_z, head_weight, preferred_element_type=jnp.float32)
    exponent = jnp.exp(logits - jnp.max(logits, axis=-1, keepdims=True))
    probability = exponent / jnp.sum(exponent, axis=-1, keepdims=True)
    onehot = (targets[:, None] == lax.broadcasted_iota(jnp.int32, logits.shape, 1)).astype(
        jnp.float32
    )
    grad_logits = ((probability - onehot) * keep_mask[:, None]).astype(jnp.bfloat16)
    return (
        contract(grad_logits, head_weight, 1, 1).astype(jnp.bfloat16),
        contract(rounded_z, grad_logits, 0, 0),
    )


def second_step(pair_one, targets, live_mask, gain_second, second_in, second_out, head_weight):
    start_f = pair_one.astype(jnp.float32)
    delta, saved = transition_forward(start_f, gain_second, second_in, second_out)
    rounded_z = (start_f + live_mask[:, None] * delta).astype(jnp.bfloat16)
    grad_two, head_part = head_step(rounded_z, targets, jnp.ones_like(live_mask), head_weight)
    masked_out = jnp.where(live_mask[:, None] > 0, grad_two, jnp.zeros((), jnp.bfloat16))
    back_field, in_part, out_part = transition_backward(
        saved, masked_out, gain_second, second_in, second_out, True
    )
    return (
        (grad_two.astype(jnp.float32) + back_field).astype(jnp.bfloat16),
        in_part,
        out_part,
        head_part,
    )


def local(
    singles,
    pair_in,
    proj_weight,
    gain_first,
    first_in,
    first_out,
    gain_second,
    second_in,
    second_out,
    head_weight,
    pae_bins,
    chain_perm,
    resolved_counts,
    tile_order,
):
    rows_dev, cols_dev, width = pair_in.shape
    tile_len = TILE
    tiles_dev = rows_dev * cols_dev // tile_len
    token_count = chain_perm.shape[0]
    row_index = lax.axis_index("row")
    col_index = lax.axis_index("col")
    col_count = lax.axis_size("col")
    partial_proj = jnp.dot(singles, proj_weight, preferred_element_type=jnp.float32)
    projected = lax.psum(partial_proj, "col")
    left_part = projected[:, :width]
    right_part = projected[:, width:].astype(jnp.bfloat16)
    col_start = col_index * cols_dev
    right_all = lax.all_gather(right_part, "row", axis=0, tiled=True)
    col_right = lax.dynamic_slice_in_dim(right_all, col_start, cols_dev, 0)
    col_right_f = col_right.astype(jnp.float32)
    block_rows = block_size(rows_dev, cols_dev, 1024)
    row_blocks = rows_dev // block_rows
    block_pairs = block_rows * cols_dev

    def start_field(block_index):
        first_row = block_index * block_rows
        pair_rows = lax.dynamic_slice_in_dim(pair_in, first_row, block_rows, 0).astype(jnp.float32)
        left_rows = lax.dynamic_slice_in_dim(left_part, first_row, block_rows, 0)
        field_rows = pair_rows + left_rows[:, None, :] + col_right_f[None, :, :]
        return field_rows.reshape(block_pairs, width)

    def forward_block(block_index):
        start_z = start_field(block_index)
        delta, unused_saved = transition_forward(start_z, gain_first, first_in, first_out)
        return (start_z + delta).astype(jnp.bfloat16)

    block_ids = jnp.arange(row_blocks, dtype=jnp.int32)
    pair_one = lax.map(forward_block, block_ids).reshape(rows_dev * cols_dev, width)
    live_count = resolved_counts[0, col_index]
    order_list = tile_order[0]
    tile_iota = jnp.arange(tiles_dev, dtype=jnp.int32)
    rank_of = jnp.sum(
        jnp.where(order_list[None, :] == tile_iota[:, None], tile_iota[None, :], 0), axis=1
    )
    tile_live = rank_of < live_count
    pair_live = jnp.repeat(tile_live, tile_len).astype(jnp.float32)
    perm_rows = (
        lax.dynamic_slice_in_dim(chain_perm, row_index * rows_dev, rows_dev, 0)
        - row_index * rows_dev
    )
    perm_cols = lax.dynamic_slice_in_dim(chain_perm, col_start, cols_dev, 0) - col_start
    targets = jnp.take(jnp.take(pae_bins, perm_rows, axis=0), perm_cols, axis=1).reshape(
        rows_dev * cols_dev
    )
    pair_stack = pair_one.reshape(row_blocks, block_pairs, width)
    target_stack = targets.reshape(row_blocks, block_pairs)
    live_stack = pair_live.reshape(row_blocks, block_pairs)
    zero_in = jnp.zeros(second_in.shape, jnp.float32)
    zero_out = jnp.zeros(second_out.shape, jnp.float32)
    zero_head = jnp.zeros(head_weight.shape, jnp.float32)

    def head_block(running, operands):
        grad_two, head_part = head_step(operands[0], operands[1], 1.0 - operands[2], head_weight)
        return (running + head_part, grad_two)

    head_sum, rest_stack = lax.scan(head_block, zero_head, (pair_stack, target_stack, live_stack))
    rest_tiles = rest_stack.reshape(tiles_dev, tile_len, width)
    slots = -(-tiles_dev // col_count)
    row_counts = resolved_counts[0]
    offsets = jnp.cumsum(row_counts) - row_counts
    my_offset = offsets[col_index]
    worker_iota = jnp.arange(col_count, dtype=jnp.int32)[:, None]
    slot_iota = jnp.arange(slots, dtype=jnp.int32)[None, :]
    send_rank = col_count * slot_iota + jnp.mod(worker_iota - my_offset, col_count)
    send_valid = send_rank < live_count
    send_ids = order_list[jnp.minimum(send_rank, tiles_dev - 1)]
    tile_view = pair_one.reshape(tiles_dev, tile_len, width)
    target_view = targets.reshape(tiles_dev, tile_len).astype(jnp.bfloat16)
    send_pairs = jnp.where(
        send_valid[:, :, None, None], tile_view[send_ids], jnp.zeros((), jnp.bfloat16)
    )
    send_targets = jnp.where(
        send_valid[:, :, None], target_view[send_ids], jnp.zeros((), jnp.bfloat16)
    )
    recv_pairs, recv_targets = (
        lax.all_to_all(send_pairs, "col", split_axis=0, concat_axis=0, tiled=True),
        lax.all_to_all(send_targets, "col", split_axis=0, concat_axis=0, tiled=True),
    )
    work_count = tiles_dev // 2
    position = jnp.arange(work_count, dtype=jnp.int32)
    global_rank = col_count * position + col_index
    source = jnp.sum((offsets[None, :] <= global_rank[:, None]).astype(jnp.int32), axis=1) - 1
    source_slot = (global_rank - offsets[source]) // col_count
    flat_index = source * slots + source_slot
    work_pairs = recv_pairs.reshape(col_count * slots, tile_len, width)[flat_index]
    work_targets = recv_targets.reshape(col_count * slots, tile_len)[flat_index].astype(jnp.int32)
    block_tiles = block_size(work_count, tile_len, 1024)
    work_blocks = work_count // block_tiles
    work_pair_stack = work_pairs.reshape(work_blocks, block_tiles * tile_len, width)
    work_target_stack = work_targets.reshape(work_blocks, block_tiles * tile_len)

    def worker_block(running, operands):
        all_live = jnp.ones(operands[1].shape, jnp.float32)
        grad_one, in_part, out_part, head_part = second_step(
            operands[0], operands[1], all_live, gain_second, second_in, second_out, head_weight
        )
        return ((running[0] + in_part, running[1] + out_part, running[2] + head_part), grad_one)

    weight_sums, work_grad_stack = lax.scan(
        worker_block, (zero_in, zero_out, head_sum), (work_pair_stack, work_target_stack)
    )
    work_grads = work_grad_stack.reshape(work_count, tile_len, width)
    back_rank = col_count * slot_iota + jnp.mod(col_index - offsets[:, None], col_count)
    back_valid = back_rank < row_counts[:, None]
    back_position = jnp.minimum((offsets[:, None] + back_rank) // col_count, work_count - 1)
    back_pairs = jnp.where(
        back_valid[:, :, None, None], work_grads[back_position], jnp.zeros((), jnp.bfloat16)
    )
    returned = lax.all_to_all(back_pairs, "col", split_axis=0, concat_axis=0, tiled=True)
    tile_worker = jnp.mod(my_offset + rank_of, col_count)
    tile_slot = jnp.minimum(rank_of // col_count, slots - 1)
    from_worker = returned.reshape(col_count * slots, tile_len, width)[
        tile_worker * slots + tile_slot
    ]
    grad_one_all = jnp.where(tile_live[:, None, None], from_worker, rest_tiles).reshape(
        rows_dev * cols_dev, width
    )
    grad_one_stack = grad_one_all.reshape(row_blocks, block_pairs, width)

    def backward_block(running, operands):
        block_index, grad_one = operands
        start_z = start_field(block_index)
        unused_delta, saved = transition_forward(start_z, gain_first, first_in, first_out)
        back_field, unused_in, unused_out = transition_backward(
            saved, grad_one, gain_first, first_in, first_out, False
        )
        grad_zero = (grad_one.astype(jnp.float32) + back_field).reshape(block_rows, cols_dev, width)
        return (
            running + jnp.sum(grad_zero, axis=0),
            (grad_zero.astype(jnp.bfloat16), jnp.sum(grad_zero, axis=1)),
        )

    right_grad, (pair_grad_stack, left_stack) = lax.scan(
        backward_block, jnp.zeros((cols_dev, width), jnp.float32), (block_ids, grad_one_stack)
    )
    pair_grad = pair_grad_stack.reshape(rows_dev, cols_dev, width)
    left_grad = left_stack.reshape(rows_dev, width)
    token_part = jnp.zeros((token_count, 2 * width), jnp.float32)
    token_part = lax.dynamic_update_slice(token_part, left_grad, (row_index * rows_dev, 0))
    token_part = lax.dynamic_update_slice(token_part, right_grad, (col_start, width))
    token_total, in_total, out_total, head_total = lax.psum(
        (token_part, weight_sums[0], weight_sums[1], weight_sums[2]), ("row", "col")
    )
    token_rows = lax.dynamic_slice_in_dim(token_total, row_index * rows_dev, rows_dev, 0).astype(
        jnp.bfloat16
    )
    single_grad = contract(token_rows, proj_weight, 1, 1)
    return (
        pair_grad,
        single_grad,
        in_total / token_count,
        out_total / token_count,
        head_total / token_count,
    )


def solution(mesh):
    in_specs = (
        P("row", "col"),
        P("row", "col", None),
        P("col", None),
        P(),
        P(),
        P(),
        P(),
        P(),
        P(),
        P(),
        P("row", "col"),
        P(),
        P("row", None),
        P("row", "col"),
    )
    out_specs = (P("row", "col", None), P("row", "col"), P(), P(), P())
    return jax.shard_map(local, mesh=mesh, in_specs=in_specs, out_specs=out_specs, check_vma=False)
```

profile of v0, /device:TPU:1, one launch (start us, length us, event | category | flops | bytes accessed | tf_op | source)
XLA Modules:
  0.0 618.8 jit_solution(7770418198475508663)
XLA Ops:
  7.9 1.5 fusion.87
  13.8 1.9 gather_fusion.2
  21.9 7.6 %all-to-all-start.1 = ((bf16[16,2,256]{2,1,0:T(2,128)(2,1)}), bf16[16,2,256]{2,1,0:T(2,128)(2,1)S(1)}, u32[]{:S(2)}, u32[]{:S(2)}) async-start(bf16[16,2,256]{2,1,0:T(2,128)(2,1)} %reshape.938), calls=%async_computation.1 | async-start | bytes 32768 | tf_op jit(solution)/shard_map/all_to_all | solution.py:187
  30.6 10.0 %fusion.77 = s32[128]{0:T(128)S(1)} fusion(s32[128]{0:T(128)S(1)} %convert_reduce_fusion.1, s32[]{:T(128)} %bitcast.33, s32[]{:T(128)} %bitcast.34, s32[]{:T(128)} %bitcast.35, s32[]{:T(128)} %bitcast.36, s32[]{:T(128)} %bitcast.37, s32[]{:T(128)} %bitcast.39, s32[]{:T(128)} %bitcast.38, s32[]{:T(128)} %bitcast.16, s32[]{:T(128)} %bitcast.18, s32[]{:T(128)} %bitcast.20, ...), kind=kLoop, calls=%fused_computation.208 | loop fusion | flops 7296 | bytes 1092 | tf_op jit(solution)/shard_map/select_n | solution.py:195
  42.0 54.0 %all-reduce.6.cloned.1.call-done = f32[128,256]{1,0:T(8,128)} async-done(((f32[128,256]{1,0:T(8,128)}), f32[128,256]{1,0:T(8,128)}) %all-reduce.6.cloned.1.call-update) | async-done | bytes 131088 | tf_op jit(solution)/shard_map/psum | solution.py:114
  96.8 15.6 %all_gather.3 = bf16[1024,128]{1,0:T(8,128)(2,1)S(1)} all-gather(bf16[128,128]{1,0:T(8,128)(2,1)S(1)} %slice.95), channel_id=1, replica_groups=mesh['row'=8,'col'=16] {'row'}, dimensions={0}, use_global_device_ids=true | all-gather | bytes 294912 | tf_op jit(solution)/shard_map/all_gather | solution.py:118
  112.5 1.5 slice.72
  113.9 1.6 broadcast.784.clone
  115.5 64.0 %while.55 = (s32[]{:T(128)}, bf16[8,1024,128]{2,1,0:T(8,128)(2,1)}, s32[8]{0:T(128)S(1)}, bf16[128,64,128]{2,1,0:T(8,128)(2,1)}, f32[128,128]{1,0:T(8,128)}, /*i...) while((s32[]{:T(128)}, bf16[8,1024,128]{2,1,0:T(8,128)(2,1)}, ...), condition=%wide.region_6.7_spmd, body=%wide.region_3.6_spmd.sunk | while | flops 407897088 | bytes 11818179 | solution.py:138
  121.2 2.3 fusion.163
  129.2 2.3 fusion.163
  137.2 2.3 fusion.163
  145.2 2.3 fusion.163
  153.2 2.3 fusion.163
  161.2 2.3 fusion.163
  169.2 2.3 fusion.163
  177.2 2.3 fusion.163
  179.6 2.6 gather_fusion.3
  182.2 1.6 broadcast_select_fusion
  183.7 4.8 all-to-all-start
  189.2 22.2 %while.56 = (s32[]{:T(128)}, f32[128,64]{0,1:T(8,128)S(1)}, bf16[8,1024,128]{2,1,0:T(8,128)(2,1)S(1)}, bf16[8,1024,128]{2,1,0:T(8,128)(2,1)}, bf16[128,64]{0,1:T...) while((s32[]{:T(128)}, f32[128,64]{0,1:T(8,128)S(1)}, ...), condition=%wide.region_10.11_spmd.clone, body=%wide.region_7.10_spmd.clone.sunk | while | flops 51592192 | bytes 1995891 | solution.py:166
  211.5 9.9 %all-to-all-done = bf16[16,16,32,128]{3,2,1,0:T(8,128)(2,1)} async-done(((bf16[16,16,32,128]{3,2,1,0:T(8,128)(2,1)}), bf16[16,16,32,128]{3,2,1,0:T(8,128)(2,1)}, u32[]{:S(2)}, u32[]{:S(2)}) %all-to-all-start) | async-done | bytes 2097184 | tf_op jit(solution)/shard_map/all_to_all | solution.py:186
  221.4 2.4 gather_fusion.4
  223.8 45.5 %while.57 = (s32[]{:T(128)}, f32[128,1024]{1,0:T(8,128)}, f32[512,128]{1,0:T(8,128)S(1)}, f32[128,64]{0,1:T(8,128)S(1)}, bf16[4,1024,128]{2,1,0:T(8,128)(2,1)}, ...) while((s32[]{:T(128)}, f32[128,1024]{1,0:T(8,128)}, ...), condition=%wide.region_19.20_spmd.clone, body=%wide.region_12.19_spmd.clone.sunk | while | flops 1282874368 | bytes 39037144 | solution.py:209
  231.5 3.5 fusion.189
  242.8 3.7 fusion.189
  254.2 3.7 fusion.189
  265.6 3.7 fusion.189
  269.3 2.3 gather_fusion.7
  271.6 1.5 broadcast_select_fusion.1
  273.2 3.7 all-to-all-start.2
  278.3 161.1 %all-reduce.8.cloned.1.call-done = (f32[128,1024]{1,0:T(8,128)}, f32[512,128]{1,0:T(8,128)}) async-done(((f32[128,1024]{1,0:T(8,128)}, f32[512,128]{1,0:T(8,128)}), (f32[128,1024]{1,0:T(8,128)}, f32[512,128]{1,0:T(8,128)})) %all-reduce.8.cloned.1.call-update) | async-done | bytes 786448 | tf_op jit(solution)/shard_map/psum | solution.py:251
  439.5 1.7 broadcast_multiply_fusion.8
  441.1 1.9 broadcast_multiply_fusion.7
  443.0 2.2 gather_fusion.8
  445.2 3.6 bitcast_select_fusion
  448.7 89.8 %while.58 = (s32[]{:T(128)}, f32[64,128]{1,0:T(8,128)S(1)}, bf16[8,16,64,128]{3,2,1,0:T(8,128)(2,1)}, f32[8,16,128]{2,1,0:T(8,128)}, bf16[8,1024,128]{2,1,0:T(8,...) while((s32[]{:T(128)}, f32[64,128]{1,0:T(8,128)S(1)}, ...), condition=%wide.region_27.28_spmd.clone, body=%wide.region_20.27_spmd.clone.sunk | while | flops 686169088 | bytes 20674808 | solution.py:243
  454.5 2.0 fusion.198
  465.7 2.0 fusion.198
  476.9 2.0 fusion.198
  479.0 1.4 fusion.199
  488.2 2.0 fusion.198
  499.4 2.0 fusion.198
  510.6 2.0 fusion.198
  521.8 2.0 fusion.198
  533.0 2.0 fusion.198
  535.1 1.4 fusion.199
  539.5 71.1 %all-reduce.9 = (bf16[1024,256]{1,0:T(8,128)(2,1)S(1)}, f32[128,64]{0,1:T(8,128)S(1)}) all-reduce(f32[1024,256]{1,0:T(8,128)S(1)} %constant_dynamic-update-slice_fusion.2, f32[128,64]{0,1:T(8,128)S(1)} %get-tuple-element.223), channel_id=1, replica_groups=mesh['row'=8,'col'=16] {'row','col'}, use_global_device_ids=true, to_apply=%region_28.29 | all-reduce | flops 270336 | bytes 1638400 | tf_op jit(solution)/shard_map/psum | solution.py:251
  (456 shorter events, 175.5 us)
Async XLA Ops:
  7.2 0.7 copy-start
  7.2 6.6 %copy-start.1 = (s32[1,256]{1,0:T(1,128)S(1)}, s32[1,256]{1,0:T(1,128)}, u32[]{:S(2)}) copy-start(s32[1,256]{1,0:T(1,128)} %param.35) | copy-start | bytes 3076
  7.2 88.8 %all-reduce.6.cloned.1.call-start = ((), (), s32[]{:S(2)}) async-start(), calls=%async_computation.3 | async-start | bytes 262144 | tf_op jit(solution)/shard_map/psum | solution.py:114
  13.8 3.7 copy-start.9
  13.8 5.6 copy-start.11
  20.2 95.3 %copy-start.2 = (bf16[128,1024]{1,0:T(8,128)(2,1)S(1)}, bf16[128,1024]{1,0:T(8,128)(2,1)}, u32[]{:S(2)}) copy-start(bf16[128,1024]{1,0:T(8,128)(2,1)} %param.26) | copy-start | bytes 786436
  20.2 95.3 %copy-start.8 = (f32[128]{0:T(128)S(1)}, f32[128]{0:T(128)}, u32[]{:S(2)}) copy-start(f32[128]{0:T(128)} %param.25) | copy-start | bytes 1540
  21.9 19.1 %all-to-all-start.1 = ((bf16[16,2,256]{2,1,0:T(2,128)(2,1)}), bf16[16,2,256]{2,1,0:T(2,128)(2,1)S(1)}, u32[]{:S(2)}, u32[]{:S(2)}) async-start(bf16[16,2,256]{2,1,0:T(2,128)(2,1)} %reshape.938), calls=%async_computation.1 | async-start | bytes 32768 | tf_op jit(solution)/shard_map/all_to_all | solution.py:187
  183.7 37.7 %all-to-all-start = ((bf16[16,16,32,128]{3,2,1,0:T(8,128)(2,1)}), bf16[16,16,32,128]{3,2,1,0:T(8,128)(2,1)}, u32[]{:S(2)}, u32[]{:S(2)}) async-start(bf16[16,16,32,128]{3,2,1,0:T(8,128)(2,1)} %broadcast_select_fusion), calls=%async_computation | async-start | bytes 4194304 | tf_op jit(solution)/shard_map/all_to_all | solution.py:186
  188.5 0.7 copy-start.7
  211.4 10.0 %copy-start.4 = (bf16[8,1024,128]{2,1,0:T(8,128)(2,1)}, bf16[8,1024,128]{2,1,0:T(8,128)(2,1)S(1)}, u32[]{:S(2)}) copy-start(bf16[8,1024,128]{2,1,0:T(8,128)(2,1)S(1)} %get-tuple-element.217) | copy-start | bytes 6291460
  211.4 12.3 %copy-start.5 = (bf16[128,1024]{1,0:T(8,128)(2,1)S(1)}, bf16[128,1024]{1,0:T(8,128)(2,1)}, u32[]{:S(2)}) copy-start(bf16[128,1024]{1,0:T(8,128)(2,1)} %param.29) | copy-start | bytes 786436
  211.4 12.3 %copy-start.6 = (bf16[512,128]{1,0:T(8,128)(2,1)S(1)}, bf16[512,128]{1,0:T(8,128)(2,1)}, u32[]{:S(2)}) copy-start(bf16[512,128]{1,0:T(8,128)(2,1)} %param.30) | copy-start | bytes 393220
  211.4 12.3 %copy-start.10 = (f32[128]{0:T(128)S(1)}, f32[128]{0:T(128)}, u32[]{:S(2)}) copy-start(f32[128]{0:T(128)} %param.28) | copy-start | bytes 1540
  228.1 1.4 copy-start.12
  228.1 1.4 copy-start.13
  239.4 1.4 copy-start.12
  239.4 1.4 copy-start.13
  250.8 1.4 copy-start.12
  250.8 1.4 copy-start.13
  262.2 1.4 copy-start.12
  262.2 1.4 copy-start.13
  269.3 2.3 copy-start.3
  273.2 169.8 %all-to-all-start.2 = ((bf16[16,16,32,128]{3,2,1,0:T(8,128)(2,1)}), bf16[16,16,32,128]{3,2,1,0:T(8,128)(2,1)S(1)}, u32[]{:S(2)}, u32[]{:S(2)}) async-start(bf16[16,16,32,128]{3,2,1,0:T(8,128)(2,1)} %broadcast_select_fusion.1), calls=%async_computation.2 | async-start | bytes 4194304 | tf_op jit(solution)/shard_map/all_to_all | solution.py:219
  276.9 162.6 %all-reduce.8.cloned.1.call-start = ((), (), s32[]{:S(2)}) async-start(), calls=%async_computation.4 | async-start | bytes 1572864 | tf_op jit(solution)/shard_map/psum | solution.py:251
Sparse Core Ops, SparseCore 0:
  11.8 84.1 all-reduce.5
  283.0 156.3 all-reduce.7
where the time goes:
time: 623 us; the launch traced here: 619 us
  waiting for transfers between devices  226 us (36%)
  matrix products  115 us (18%)
  other arithmetic  88.6 us (14%)
  blocking collectives  86.8 us (14%)
  local copies, waits for them, and re-layouts  58.9 us (9%)
  starting transfers between devices  16.4 us (3%)
  between operations  14.5 us (2%)
  loops' own time  12.6 us (2%)
    psum x1, waiting for transfers between devices, local(): lax.psum((token_part, weight_sums[0], weight_sums[1], weight_sums[2]), ('...  161 us
    psum x1, blocking collectives, local(): lax.psum((token_part, weight_sums[0], weight_sums[1], weight_sums[2]), ('...  71.1 us
    dot_general x57, matrix products, contract(): lax.dot_general(left_op, right_op, (((left_dim,), (right_dim,)), ((), ())...  68 us
    psum x1, waiting for transfers between devices, local(): projected = lax.psum(partial_proj, 'col')  54 us
    reduce_sum x20, other arithmetic, transition_forward(): jnp.mean(centred * centred, axis=-1, keepdims=True) + 1e-05  23.1 us
    dot_general x12, matrix products, transition_forward(): result = jnp.dot(hidden_act, w_out, preferred_element_type=jnp.float32)  20.6 us
    reduce_sum x20, other arithmetic, transition_forward(): average = jnp.mean(start_z, axis=-1, keepdims=True)  19.2 us
    all_gather x1, blocking collectives, local(): right_all = lax.all_gather(right_part, 'row', axis=0, tiled=True)  15.6 us
  transfers between devices with their start and end apart: 5, of which 3 were waited for; matrix products, arithmetic and copies ran while one was open for 8% of the time, Pallas kernels for 0%

commit v1 on v0

--- a/solution.py
+++ b/solution.py
@@ -111,7 +111,7 @@
     col_index = lax.axis_index("col")
     col_count = lax.axis_size("col")
     partial_proj = jnp.dot(singles, proj_weight, preferred_element_type=jnp.float32)
-    projected = lax.psum(partial_proj, "col")
+    projected = jnp.sum(lax.all_gather(partial_proj, "col"), axis=0)
     left_part = projected[:, :width]
     right_part = projected[:, width:].astype(jnp.bfloat16)
     col_start = col_index * cols_dev

time: 623 us -> 568 us (0.912)
  waiting for transfers between devices: 226 us -> 187 us
  local copies, waits for them, and re-layouts: 58.9 us -> 39.9 us
  other arithmetic: 88.6 us -> 99.8 us
  matrix products: 115 us -> 108 us
    psum x1 -> x0, waiting for transfers between devices: 54 us -> none  [local(): projected = lax.psum(partial_proj, 'col')]
    all_gather x0 -> x1, waiting for transfers between devices: none -> 15.2 us  [local(): projected = jnp.sum(lax.all_gather(partial_proj, 'col'), axis=0)]
    dynamic_slice x16, local copies, waits for them, and re-layouts: 11.3 us -> 0.13 us  [start_field(): left_rows = lax.dynamic_slice_in_dim(left_part, first_row, block_rows, 0)]
    reduce_sum x8, other arithmetic: 4.99 us -> 12.8 us  [backward_block(): jnp.sum(grad_zero, axis=1)]
    dot_general x12, matrix products: 20.6 us -> 13.3 us  [transition_forward(): result = jnp.dot(hidden_act, w_out, preferred_element_type=jnp.float32)]
  transfers between devices with their start and end apart: 5 -> 5, of which waited for: 3 -> 3; matrix products, arithmetic and copies ran while one was open for 8% -> 9% of each run, Pallas kernels for 0% -> 0%
where the time goes in v1:
time: 568 us; the launch traced here: 565 us
  waiting for transfers between devices  187 us (33%)
  matrix products  108 us (19%)
  other arithmetic  99.8 us (18%)
  blocking collectives  86.5 us (15%)
  local copies, waits for them, and re-layouts  39.9 us (7%)
  starting transfers between devices  16.3 us (3%)
  between operations  14.5 us (3%)
  loops' own time  12.7 us (2%)
    psum x1, waiting for transfers between devices, local(): lax.psum((token_part, weight_sums[0], weight_sums[1], weight_sums[2]), ('...  161 us
    psum x1, blocking collectives, local(): lax.psum((token_part, weight_sums[0], weight_sums[1], weight_sums[2]), ('...  71.1 us
    dot_general x57, matrix products, contract(): lax.dot_general(left_op, right_op, (((left_dim,), (right_dim,)), ((), ())...  68.3 us
    reduce_sum x20, other arithmetic, transition_forward(): jnp.mean(centred * centred, axis=-1, keepdims=True) + 1e-05  23.1 us
    reduce_sum x20, other arithmetic, transition_forward(): average = jnp.mean(start_z, axis=-1, keepdims=True)  19.3 us
    all_gather x1, blocking collectives, local(): right_all = lax.all_gather(right_part, 'row', axis=0, tiled=True)  15.4 us
    all_gather x1, waiting for transfers between devices, local(): projected = jnp.sum(lax.all_gather(partial_proj, 'col'), axis=0)  15.2 us
    dot_general x20, matrix products, transition_forward(): gate_up = jnp.dot(inputs, w_in, preferred_element_type=jnp.float32)  15.1 us
  transfers between devices with their start and end apart: 5, of which 3 were waited for; matrix products, arithmetic and copies ran while one was open for 9% of the time, Pallas kernels for 0%

profile of v1, /device:TPU:1, one launch (start us, length us, event | category | flops | bytes accessed | tf_op | source)
XLA Modules:
  0.0 565.0 jit_solution(3548427550902303094)
XLA Ops:
  7.9 1.5 fusion.87
  13.9 1.9 gather_fusion.2
  21.9 7.6 %all-to-all-start.1 = ((bf16[16,2,256]{2,1,0:T(2,128)(2,1)}), bf16[16,2,256]{2,1,0:T(2,128)(2,1)S(1)}, u32[]{:S(2)}, u32[]{:S(2)}) async-start(bf16[16,2,256]{2,1,0:T(2,128)(2,1)} %reshape.939), calls=%async_computation.1 | async-start | bytes 32768 | tf_op jit(solution)/shard_map/all_to_all | solution.py:187
  29.9 10.0 %fusion.77 = s32[128]{0:T(128)S(1)} fusion(s32[128]{0:T(128)S(1)} %convert_reduce_fusion.1, s32[]{:T(128)} %bitcast.34, s32[]{:T(128)} %bitcast.35, s32[]{:T(128)} %bitcast.36, s32[]{:T(128)} %bitcast.37, s32[]{:T(128)} %bitcast.38, s32[]{:T(128)} %bitcast.40, s32[]{:T(128)} %bitcast.39, s32[]{:T(128)} %bitcast.17, s32[]{:T(128)} %bitcast.19, s32[]{:T(128)} %bitcast.21, ...), kind=kLoop, calls=%fused_computation.208 | loop fusion | flops 7296 | bytes 1092 | tf_op jit(solution)/shard_map/select_n | solution.py:195
  42.0 15.2 %all-gather.3.cloned.1.call-done = f32[2048,256]{1,0:T(8,128)} async-done(((f32[128,256]{1,0:T(8,128)}), f32[2048,256]{1,0:T(8,128)}) %all-gather.3.cloned.1.call-update) | async-done | bytes 2097168 | tf_op jit(solution)/shard_map/all_gather | solution.py:114
  57.3 1.8 reduce_sum.156
  59.1 15.4 %all_gather.11 = bf16[1024,128]{1,0:T(8,128)(2,1)S(1)} all-gather(bf16[128,128]{1,0:T(8,128)(2,1)S(1)} %slice.95), channel_id=1, replica_groups=mesh['row'=8,'col'=16] {'row'}, dimensions={0}, use_global_device_ids=true | all-gather | bytes 294912 | tf_op jit(solution)/shard_map/all_gather | solution.py:118
  74.4 1.6 broadcast.784.clone
  76.0 51.3 %while.55 = (s32[]{:T(128)}, bf16[8,1024,128]{2,1,0:T(8,128)(2,1)}, s32[8]{0:T(128)S(1)}, bf16[128,64,128]{2,1,0:T(8,128)(2,1)}, f32[128,128]{1,0:T(8,128)S(1)},...) while((s32[]{:T(128)}, bf16[8,1024,128]{2,1,0:T(8,128)(2,1)}, ...), condition=%wide.region_6.7_spmd, body=%wide.region_3.6_spmd.sunk | while | flops 407897088 | bytes 11818179 | solution.py:138
  81.0 1.4 fusion.163
  87.5 1.4 fusion.163
  127.4 2.6 gather_fusion.3
  130.0 1.6 broadcast_select_fusion
  131.5 4.7 all-to-all-start
  137.0 22.1 %while.56 = (s32[]{:T(128)}, f32[128,64]{0,1:T(8,128)S(1)}, bf16[8,1024,128]{2,1,0:T(8,128)(2,1)S(1)}, bf16[8,1024,128]{2,1,0:T(8,128)(2,1)}, bf16[128,64]{0,1:T...) while((s32[]{:T(128)}, f32[128,64]{0,1:T(8,128)S(1)}, ...), condition=%wide.region_10.11_spmd.clone, body=%wide.region_7.10_spmd.clone.sunk | while | flops 51592192 | bytes 1995891 | solution.py:166
  159.2 10.0 %all-to-all-done = bf16[16,16,32,128]{3,2,1,0:T(8,128)(2,1)} async-done(((bf16[16,16,32,128]{3,2,1,0:T(8,128)(2,1)}), bf16[16,16,32,128]{3,2,1,0:T(8,128)(2,1)}, u32[]{:S(2)}, u32[]{:S(2)}) %all-to-all-start) | async-done | bytes 2097184 | tf_op jit(solution)/shard_map/all_to_all | solution.py:186
  169.1 2.4 gather_fusion.4
  171.5 45.5 %while.57 = (s32[]{:T(128)}, f32[128,1024]{1,0:T(8,128)}, f32[512,128]{1,0:T(8,128)S(1)}, f32[128,64]{0,1:T(8,128)S(1)}, bf16[4,1024,128]{2,1,0:T(8,128)(2,1)}, ...) while((s32[]{:T(128)}, f32[128,1024]{1,0:T(8,128)}, ...), condition=%wide.region_19.20_spmd.clone, body=%wide.region_12.19_spmd.clone.sunk | while | flops 1282874368 | bytes 39037144 | solution.py:209
  179.3 3.5 fusion.189
  190.6 3.7 fusion.189
  202.0 3.7 fusion.189
  213.4 3.7 fusion.189
  217.1 2.3 gather_fusion.7
  219.4 1.5 broadcast_select_fusion.1
  220.9 3.7 all-to-all-start.2
  226.2 161.1 %all-reduce.5.cloned.1.call-done = (f32[128,1024]{1,0:T(8,128)}, f32[512,128]{1,0:T(8,128)}) async-done(((f32[128,1024]{1,0:T(8,128)}, f32[512,128]{1,0:T(8,128)}), (f32[128,1024]{1,0:T(8,128)}, f32[512,128]{1,0:T(8,128)})) %all-reduce.5.cloned.1.call-update) | async-done | bytes 786448 | tf_op jit(solution)/shard_map/psum | solution.py:251
  387.2 1.7 broadcast_multiply_fusion.8
  388.9 1.9 broadcast_multiply_fusion.7
  390.8 2.2 gather_fusion.8
  392.9 4.8 bitcast_select_fusion
  397.8 87.8 %while.58 = (s32[]{:T(128)}, f32[64,128]{1,0:T(8,128)S(1)}, bf16[8,16,64,128]{3,2,1,0:T(8,128)(2,1)}, f32[8,16,128]{2,1,0:T(8,128)S(1)}, bf16[8,1024,128]{2,1,0:...) while((s32[]{:T(128)}, f32[64,128]{1,0:T(8,128)S(1)}, ...), condition=%wide.region_27.28_spmd.clone, body=%wide.region_20.27_spmd.clone.sunk | while | flops 686169088 | bytes 20674808 | solution.py:243
  402.8 2.1 fusion.198
  406.3 1.6 bitcast_reduce_fusion.2
  413.8 2.1 fusion.198
  417.3 1.6 bitcast_reduce_fusion.2
  424.8 2.1 fusion.198
  428.2 1.6 bitcast_reduce_fusion.2
  435.7 2.1 fusion.198
  439.2 1.6 bitcast_reduce_fusion.2
  446.7 2.1 fusion.198
  450.2 1.6 bitcast_reduce_fusion.2
  457.7 2.1 fusion.198
  461.2 1.6 bitcast_reduce_fusion.2
  468.7 2.1 fusion.198
  472.1 1.6 bitcast_reduce_fusion.2
  479.6 2.1 fusion.198
  483.1 1.6 bitcast_reduce_fusion.2
  485.7 71.1 %all-reduce.6 = (bf16[1024,256]{1,0:T(8,128)(2,1)S(1)}, f32[128,64]{0,1:T(8,128)S(1)}) all-reduce(f32[1024,256]{1,0:T(8,128)S(1)} %constant_dynamic-update-slice_fusion.2, f32[128,64]{0,1:T(8,128)S(1)} %get-tuple-element.223), channel_id=1, replica_groups=mesh['row'=8,'col'=16] {'row','col'}, use_global_device_ids=true, to_apply=%region_28.29 | all-reduce | flops 270336 | bytes 1638400 | tf_op jit(solution)/shard_map/psum | solution.py:251
  (461 shorter events, 164.4 us)
Async XLA Ops:
  7.2 0.7 copy-start
  7.2 6.7 %copy-start.1 = (s32[1,256]{1,0:T(1,128)S(1)}, s32[1,256]{1,0:T(1,128)}, u32[]{:S(2)}) copy-start(s32[1,256]{1,0:T(1,128)} %param.35) | copy-start | bytes 3076
  7.2 50.1 %all-gather.3.cloned.1.call-start = ((), (), s32[]{:S(2)}) async-start(), calls=%async_computation.3 | async-start | bytes 2228224 | tf_op jit(solution)/shard_map/all_gather | solution.py:114
  13.8 2.1 copy-start.9
  15.8 4.6 copy-start.11
  21.9 19.1 %all-to-all-start.1 = ((bf16[16,2,256]{2,1,0:T(2,128)(2,1)}), bf16[16,2,256]{2,1,0:T(2,128)(2,1)S(1)}, u32[]{:S(2)}, u32[]{:S(2)}) async-start(bf16[16,2,256]{2,1,0:T(2,128)(2,1)} %reshape.939), calls=%async_computation.1 | async-start | bytes 32768 | tf_op jit(solution)/shard_map/all_to_all | solution.py:187
  57.2 18.8 %copy-start.2 = (bf16[128,1024]{1,0:T(8,128)(2,1)S(1)}, bf16[128,1024]{1,0:T(8,128)(2,1)}, u32[]{:S(2)}) copy-start(bf16[128,1024]{1,0:T(8,128)(2,1)} %param.26) | copy-start | bytes 786436
  57.2 18.8 %copy-start.8 = (f32[128]{0:T(128)S(1)}, f32[128]{0:T(128)}, u32[]{:S(2)}) copy-start(f32[128]{0:T(128)} %param.25) | copy-start | bytes 1540
  57.3 18.8 %copy-start.12 = (bf16[512,128]{1,0:T(8,128)(2,1)S(1)}, bf16[512,128]{1,0:T(8,128)(2,1)}, u32[]{:S(2)}) copy-start(bf16[512,128]{1,0:T(8,128)(2,1)} %param.27) | copy-start | bytes 393220
  131.5 37.6 %all-to-all-start = ((bf16[16,16,32,128]{3,2,1,0:T(8,128)(2,1)}), bf16[16,16,32,128]{3,2,1,0:T(8,128)(2,1)}, u32[]{:S(2)}, u32[]{:S(2)}) async-start(bf16[16,16,32,128]{3,2,1,0:T(8,128)(2,1)} %broadcast_select_fusion), calls=%async_computation | async-start | bytes 4194304 | tf_op jit(solution)/shard_map/all_to_all | solution.py:186
  136.3 0.7 copy-start.7
  159.1 10.0 %copy-start.4 = (bf16[8,1024,128]{2,1,0:T(8,128)(2,1)}, bf16[8,1024,128]{2,1,0:T(8,128)(2,1)S(1)}, u32[]{:S(2)}) copy-start(bf16[8,1024,128]{2,1,0:T(8,128)(2,1)S(1)} %get-tuple-element.217) | copy-start | bytes 6291460
  159.1 12.4 %copy-start.5 = (bf16[128,1024]{1,0:T(8,128)(2,1)S(1)}, bf16[128,1024]{1,0:T(8,128)(2,1)}, u32[]{:S(2)}) copy-start(bf16[128,1024]{1,0:T(8,128)(2,1)} %param.29) | copy-start | bytes 786436
  159.2 12.4 %copy-start.6 = (bf16[512,128]{1,0:T(8,128)(2,1)S(1)}, bf16[512,128]{1,0:T(8,128)(2,1)}, u32[]{:S(2)}) copy-start(bf16[512,128]{1,0:T(8,128)(2,1)} %param.30) | copy-start | bytes 393220
  159.2 12.4 %copy-start.10 = (f32[128]{0:T(128)S(1)}, f32[128]{0:T(128)}, u32[]{:S(2)}) copy-start(f32[128]{0:T(128)} %param.28) | copy-start | bytes 1540
  175.9 1.4 copy-start.14
  175.9 1.4 copy-start.15
  187.1 1.4 copy-start.14
  187.2 1.4 copy-start.15
  198.6 1.4 copy-start.14
  198.6 1.4 copy-start.15
  210.0 1.4 copy-start.14
  210.0 1.4 copy-start.15
  217.1 2.3 copy-start.3
  220.9 169.8 %all-to-all-start.2 = ((bf16[16,16,32,128]{3,2,1,0:T(8,128)(2,1)}), bf16[16,16,32,128]{3,2,1,0:T(8,128)(2,1)S(1)}, u32[]{:S(2)}, u32[]{:S(2)}) async-start(bf16[16,16,32,128]{3,2,1,0:T(8,128)(2,1)} %broadcast_select_fusion.1), calls=%async_computation.2 | async-start | bytes 4194304 | tf_op jit(solution)/shard_map/all_to_all | solution.py:219
  224.7 162.6 %all-reduce.5.cloned.1.call-start = ((), (), s32[]{:S(2)}) async-start(), calls=%async_computation.4 | async-start | bytes 1572864 | tf_op jit(solution)/shard_map/psum | solution.py:251
  392.9 4.8 copy-start.13
Sparse Core Ops, SparseCore 0:
  10.7 46.4 all-gather.2
  230.8 156.3 all-reduce.4
